TPU v7x, 512 devices: a whole 4x4x16 slice. The times are simulated.
512 devices in a mesh: seq: 64 (over x, z), head: 8 (over y, core).
Axes of the slice: x: 4, y: 4, z: 16, core: 2. Of those that a mesh axis runs over, the one named last changes fastest.
Arguments:
- qk: bfloat16 [8, 32768, 128], P('head', 'seq'), may hold values from -32 to 32
- values: bfloat16 [8, 32768, 128], P('head', 'seq'), may hold values from -6 to 6
- grad_out: bfloat16 [8, 32768, 128], P('head', 'seq'), may hold values from -6 to 6
- members: int32 [8, 2, 192, 256], P('head'), may hold values from 0 to 32767, as said below
- counts: int32 [8, 2, 192], P('head'), may hold values from 1 to 256, as said below
Outputs:
- d_qk: bfloat16 [8, 32768, 128], P('head', 'seq')
- d_values: bfloat16 [8, 32768, 128], P('head', 'seq')
Inputs may be any that keep to these rules, and one draw needn't show every extreme that they name: `members`: for each head and round, every token index is in exactly one valid slot; the valid slots of a group are its first counts ones and hold increasing tokens, other slots hold any token. The 3 groups c with c // 3 equal hold at most 16 valid slots whose tokens t have one value of t // 512. For each head and round the counts sum to 32768.
All inputs are finite; a program needn't handle non-finite values.
Results may differ from a plain program's by a relative error of at most 0.012.
Values may be sent and summed in bfloat16 or wider, within the bound.
A program may use at most 64 MiB of HBM per device.

v0:
```python
import functools

import jax
import jax.numpy as jnp
from jax import lax
from jax.experimental import pallas as pl
from jax.experimental.pallas import tpu as pltpu
from jax.sharding import PartitionSpec as P

MESH = pl.DeviceIdType.MESH
F32 = jnp.float32
BF16 = jnp.bfloat16
masked_score = -1e30
norm_eps = 1e-06
NZ = 16
NN = (((1,), (0,)), ((), ()))
NT = (((1,), (1,)), ((), ()))
TN = (((0,), (0,)), ((), ()))


def mm(a, b, dims=NN, precision=None):
    return lax.dot_general(a, b, dims, precision=precision, preferred_element_type=F32)


def iota(shape, axis):
    return lax.broadcasted_iota(jnp.int32, shape, axis)


def kernel(
    n, bound, members_hbm, counts_hbm, q_hbm, v_hbm, g_hbm, dq_ref, dv_ref,
    members_ref, counts_ref, q_ref, v_ref, g_ref, sq, rq, sg, rg, sx, rx, sy, ry, se, re, sb, rb,
    ones_s, ones_o, upper, hit_t, hit_s, lane_t, lane_s, kv, gs, unit, prob, pdc, d_unit, d_value, d_query,
    send_sem, recv_sem, near_send, near_recv, load_sem, turn,
):
    me = lax.axis_index("seq")
    head = lax.axis_index("head")
    core = lax.rem(head, 2)
    tokens, feat = q_ref.shape
    rounds = sq.shape[0]
    _, groups, cap = members_hbm.shape
    per = groups // n
    slots = per * cap
    rows = n * bound
    nx = n // NZ
    following = lax.rem(me + 1, n)
    previous = lax.rem(me + n - 1, n)

    loads = [
        pltpu.make_async_copy(src, dst, load_sem.at[i])
        for i, (src, dst) in enumerate(
            (
                *(
                    (members_hbm.at[:, :, pl.ds(h * 128, 128)], members_ref.at[h])
                    for h in range(cap // 128)
                ),
                (counts_hbm, counts_ref), (q_hbm, q_ref), (v_hbm, v_ref), (g_hbm, g_ref),
            )
        )
    ]
    for load in loads:
        load.start()
    columns = [lax.rem(lax.div(me, NZ) + dx, nx) * NZ for dx in range(nx)]

    def every_peer(act):
        def ring(a, carry):
            dz = NZ // 2 + lax.div(a + 1, 2) * (1 - 2 * lax.rem(a, 2))
            z = lax.rem(me + dz, NZ)
            for dx in range(nx):
                act(columns[dx] + z)
            return carry

        lax.fori_loop(0, NZ - 1, ring, 0)
        for dx in range(1, nx):
            act(columns[dx] + lax.rem(me, NZ))

    barrier = pltpu.get_barrier_semaphore()
    every_peer(
        lambda to: pl.semaphore_signal(
            barrier, inc=1, device_id={"seq": to}, device_id_type=MESH
        )
    )
    other = {"seq": me, "head": head + 1 - 2 * core}
    pl.semaphore_signal(barrier, inc=1, device_id=other, device_id_type=MESH)

    def spread(src, dst, idx):
        def one(to):
            pltpu.make_async_remote_copy(
                src_ref=src.at[to],
                dst_ref=dst.at[me],
                send_sem=send_sem.at[idx],
                recv_sem=recv_sem.at[idx],
                device_id={"seq": to},
                device_id_type=MESH,
            ).start()

        every_peer(one)
        dst[me] = src[me]

    def arrived(dst, idx):
        part = dst.at[pl.ds(0, n - 1)]
        pltpu.make_async_copy(part, part, recv_sem.at[idx]).wait()

    def left(src, idx):
        part = src.at[pl.ds(0, n - 1)]
        pltpu.make_async_copy(part, part, send_sem.at[idx]).wait()

    def near(src, dst, idx, to):
        return pltpu.make_async_remote_copy(
            src_ref=src,
            dst_ref=dst,
            send_sem=near_send.at[idx],
            recv_sem=near_recv.at[idx],
            device_id={"seq": to},
            device_id_type=MESH,
        )

    upper[...] = jnp.where(iota((slots, slots), 0) <= iota((slots, slots), 1), 1.0, 0.0).astype(BF16)
    expand = jnp.where(lax.div(iota((rows, n), 0), bound) == iota((rows, n), 1), 1.0, 0.0).astype(BF16)
    place = (lax.rem(iota((rows, 1), 0), bound) + 1).astype(F32)
    for load in loads:
        load.wait()
    q_v = jnp.concatenate([q_ref[...], v_ref[...]], axis=1)

    def lanes_of(table):
        ranks = jnp.sum(table, axis=0, keepdims=True).astype(jnp.int32) - 1
        return jnp.where(ranks < 0, -128, ranks)

    def place_send(r):
        parts = []
        for c in range(per):
            counts = jnp.broadcast_to(counts_ref[r : r + 1, :], (n, groups))
            picked = iota((n, groups), 1) == iota((n, groups), 0) * per + c
            count = jnp.sum(jnp.where(picked, counts, 0), axis=1, keepdims=True)
            part = jnp.concatenate(
                [members_ref[h, r, pl.ds(c, n, stride=per), :] for h in range(cap // 128)], axis=1
            )
            parts.append(jnp.where(iota((n, cap), 1) < count, part, -1))
        m = jnp.concatenate(parts, axis=1)
        mine = lax.div(m + tokens, tokens) - 1 == me
        rank = mm(jnp.where(mine, 1.0, 0.0).astype(BF16), upper[...])
        rank = jnp.where(mine, rank, 0.0)
        local = (m - me * tokens + 1).astype(F32)
        token = (iota((n, tokens), 1) + 1).astype(F32)
        table = jnp.zeros((n, tokens), F32)
        for j in range(1, bound + 1):
            column = jnp.sum(jnp.where(rank == j, local, 0.0), axis=1, keepdims=True)
            table = table + jnp.where(column == token, float(j), 0.0)
        hits = jnp.where(mm(expand, table.astype(BF16)) == place, 1.0, 0.0).astype(BF16)
        ones_s[r] = hits
        return table

    for r in range(rounds):
        table = place_send(r)
        sq[r] = mm(ones_s[r], q_v).astype(BF16).reshape(n, bound, 2 * feat)
        if r == 0:
            pl.semaphore_wait(barrier, n)

        @pl.when(core == 0)
        def _():
            spread(sq.at[r], rq.at[r], r)

        hit_t[r] = jnp.where(table > 0.0, 1.0, 0.0).astype(BF16)
        lanes = lanes_of(table) + r * bound
        lane_t[:, r * tokens : (r + 1) * tokens] = jnp.where(
            iota((128, tokens), 0) == lanes, 1.0, 0.0
        ).astype(BF16)
    for r in range(rounds):
        sg[r] = mm(ones_s[r], g_ref[...]).astype(BF16).reshape(n, bound, feat)

    @pl.when(core == 0)
    def _():
        spread(sg.at[0], rg.at[0], 2)

    def own_row(r, group):
        row = jnp.concatenate(
            [members_ref[h, r, pl.ds(group, 1), :] for h in range(cap // 128)], axis=1
        )
        counts = counts_ref[r : r + 1, :]
        count = jnp.sum(jnp.where(iota((1, groups), 1) == group, counts, 0), axis=1, keepdims=True)
        return jnp.where(iota((1, cap), 1) < count, row, -1)

    fill = []
    for r in range(rounds):
        row = jnp.concatenate([own_row(r, me * per + c) for c in range(per)], axis=1)
        src = lax.div(row + tokens, tokens) - 1
        hit = iota((n, slots), 0) == src
        spot = jnp.where(hit, 1.0, 0.0).astype(BF16)
        hit_s[r] = spot
        rank = mm(spot, upper[...])
        table = jnp.where(hit, rank, 0.0)
        ones_o[r] = jnp.where(mm(expand, table.astype(BF16)) == place, 1.0, 0.0).astype(BF16)
        lanes = lanes_of(table) + r * bound
        lane_s[:, r * slots : (r + 1) * slots] = jnp.where(
            iota((128, slots), 0) == lanes, 1.0, 0.0
        ).astype(BF16)
        before = own_row(r, previous * per + per - 1)
        fill.append(jnp.where(jnp.concatenate([before, row], axis=1) >= 0, 1.0, 0.0))
    wide = (128, cap + slots)
    valid = jnp.zeros(wide, F32)
    for r in range(rounds):
        valid = jnp.where(iota(wide, 0) == r, fill[r], valid)
    valid = valid.T

    @pl.when(core == 1)
    def _():
        pl.semaphore_wait(turn, 1)
        for r in range(rounds):
            spread(sq.at[r], rq.at[r], r)
        spread(sg.at[0], rg.at[0], 2)

    def normal(k):
        k = k.astype(F32)
        return k, lax.rsqrt(jnp.sum(k * k, axis=1, keepdims=True) + norm_eps)

    def make_unit(r, lo, hi):
        k, inverse = normal(kv[r, lo:hi, :feat])
        unit[r, lo:hi, :] = (k * inverse).astype(BF16)

    for r in range(rounds):
        arrived(rq.at[r], r)
        kv[r, cap:, :] = mm(ones_o[r], rq[r].reshape(rows, 2 * feat), TN).astype(BF16)
        make_unit(r, cap, cap + slots)
        near(kv.at[r, pl.ds(slots, cap)], kv.at[r, pl.ds(0, cap)], r, following).start()
    for r in range(1, rounds):
        spread(sg.at[r], rg.at[r], 2 + r)

    keep = iota((2 * cap, cap), 0) - cap != iota((2 * cap, cap), 1)
    lse = [[None] * per for _ in range(rounds)]
    dot = [[None] * per for _ in range(rounds)]

    def scores(r, c):
        s = mm(unit[r, c * cap : (c + 2) * cap, :], kv[r, (c + 1) * cap : (c + 2) * cap, :feat], NT)
        ok = keep & (valid[c * cap : (c + 2) * cap, r : r + 1] > 0.0)
        s = jnp.where(ok, s, masked_score)
        high = jnp.max(s, axis=0, keepdims=True)
        e = jnp.exp(s - high)
        total = jnp.sum(e, axis=0, keepdims=True)
        prob[r * per + c] = e * (1.0 / total)
        lse[r][c] = high + jnp.log(total)

    def products(r, c):
        d = mm(kv[r, c * cap : (c + 2) * cap, feat:], gs[r, c * cap : (c + 1) * cap, :], NT)
        p = prob[r * per + c]
        dot[r][c] = jnp.sum(p.astype(BF16).astype(F32) * d, axis=0, keepdims=True)
        center = jnp.sum(p * d, axis=0, keepdims=True)
        pdc[r * per + c] = p * (d - center)

    for r in range(rounds):
        for c in range(1, per):
            scores(r, c)

    def look_back(r):
        near(kv.at[r, pl.ds(slots, cap)], kv.at[r, pl.ds(0, cap)], r, following).wait()
        make_unit(r, 0, cap)
        scores(r, 0)

    def cotangents(r):
        arrived(rg.at[r], 2 + r)
        gs[r] = mm(ones_o[r], rg[r].reshape(rows, feat), TN).astype(BF16)

    for r in range(rounds - 1):
        cotangents(r)
        if r == rounds - 2:
            @pl.when(core == 0)
            def _():
                pl.semaphore_signal(turn, inc=1, device_id=other, device_id_type=MESH)

        for c in range(1, per):
            products(r, c)
        look_back(r)
        products(r, 0)
    look_back(rounds - 1)
    cotangents(rounds - 1)
    for c in range(per):
        products(rounds - 1, c)

    shift = rounds * bound

    def split(x):
        high = x.astype(BF16)
        rest = x - high.astype(F32)
        mid = rest.astype(BF16)
        return high, mid, (rest - mid.astype(F32)).astype(BF16)

    def pack(hits, lanes, values):
        blocks = []
        for rows_of in values:
            parts = [split(row) for row in rows_of]
            for i in range(3):
                blocks.append(
                    jnp.concatenate([hits[r] * parts[r][i] for r in range(rounds)], axis=1)
                )
        spread_out = mm(jnp.concatenate(blocks, axis=0), lanes[...], NT)
        first, second = [
            spread_out[i : i + n] + spread_out[i + n : i + 2 * n] + spread_out[i + 2 * n : i + 3 * n]
            for i in (0, 3 * n)
        ]
        return first + pltpu.roll(second, shift, 1)

    def unpack(hits, lanes, packed):
        blocks = split(packed) + split(pltpu.roll(packed, 128 - shift, 1))
        blocks = jnp.concatenate(blocks, axis=0)
        out = [[None] * rounds for _ in range(2)]
        width = lanes.shape[1] // rounds
        for r in range(rounds):
            spots = mm(blocks, lanes[:, r * width : (r + 1) * width])
            for kind in range(2):
                i = 3 * n * kind
                found = spots[i : i + n] + spots[i + n : i + 2 * n] + spots[i + 2 * n : i + 3 * n]
                found = found * hits[r].astype(F32)
                out[kind][r] = jnp.sum(found, axis=0, keepdims=True)
        return out

    lse_rows = [jnp.concatenate(lse[r], axis=1) for r in range(rounds)]
    dot_rows = [jnp.concatenate(dot[r], axis=1) for r in range(rounds)]
    sx[:, 0, :] = pack(hit_s, lane_s, (lse_rows, dot_rows))
    spread(sx, rx, 4)
    arrived(rx, 4)
    log_tok, dot_tok = unpack(hit_t, lane_t, rx[:, 0, :])
    highest = functools.reduce(jnp.maximum, log_tok)
    exponent = [jnp.exp(x - highest) for x in log_tok]
    bottom = functools.reduce(jnp.add, exponent)
    weight = [x / bottom for x in exponent]
    mixture = functools.reduce(jnp.add, [w * d for w, d in zip(weight, dot_tok)])
    dlog = [w * (d - mixture) for w, d in zip(weight, dot_tok)]
    sy[:, 0, :] = pack(hit_t, lane_t, (weight, dlog))
    spread(sy, ry, 5)
    arrived(ry, 5)
    weight, dlog = unpack(hit_s, lane_s, ry[:, 0, :])

    def backward(r, c):
        w = weight[r][:, c * cap : (c + 1) * cap]
        p = prob[r * per + c]
        ds = (w * pdc[r * per + c] + dlog[r][:, c * cap : (c + 1) * cap] * p).astype(BF16)
        pw = (w * p).astype(BF16)
        du = mm(ds, kv[r, (c + 1) * cap : (c + 2) * cap, :feat])
        dv = mm(pw, gs[r, c * cap : (c + 1) * cap, :])
        d_query[r, c * cap : (c + 1) * cap, :] = mm(ds, unit[r, c * cap : (c + 2) * cap, :], TN)
        lo, mid, hi = c * cap, (c + 1) * cap, (c + 2) * cap
        if c == 0:
            se[r] = jnp.concatenate([du[:cap], dv[:cap]], axis=1).astype(BF16)
        else:
            d_unit[r, lo:mid, :] += du[:cap]
            d_value[r, lo:mid, :] += dv[:cap]
        d_unit[r, mid:hi, :] = du[cap:]
        d_value[r, mid:hi, :] = dv[cap:]

    for r in range(rounds):
        backward(r, 0)
    for r in range(rounds):
        near(se.at[r], re.at[r], rounds + r, previous).start()
    for r in range(rounds):
        for c in range(1, per):
            backward(r, c)
        near(se.at[r], re.at[r], rounds + r, previous).wait()
        edge = re[r].astype(F32)
        d_unit[r, slots:, :] += edge[:, :feat]
        d_value[r, slots:, :] += edge[:, feat:]
        k, inverse = normal(kv[r, cap:, :feat])
        du = d_unit[r, cap:, :]
        inner = jnp.sum(k * du, axis=1, keepdims=True)
        grad = d_query[r] + inverse * du - k * (inverse * inverse * inverse * inner)
        both = jnp.concatenate([grad, d_value[r, cap:, :]], axis=1).astype(BF16)
        sb[r] = mm(ones_o[r], both).astype(BF16).reshape(n, bound, 2 * feat)
        spread(sb.at[r], rb.at[r], 6 + r)
    total = jnp.zeros((tokens, 2 * feat), F32)
    for r in range(rounds):
        arrived(rb.at[r], 6 + r)
        total = total + mm(ones_s[r], rb[r].reshape(rows, 2 * feat), TN)
    dq_ref[...] = total[:, :feat].astype(BF16)
    dv_ref[...] = total[:, feat:].astype(BF16)
    for r in range(rounds):
        left(sq.at[r], r)
        left(sg.at[r], 2 + r)
        left(sb.at[r], 6 + r)
    left(sx, 4)
    left(sy, 5)


def on_device(qk, values, grad_out, members, counts):
    n = lax.axis_size("seq")
    _, tokens, feat = qk.shape
    _, rounds, groups, cap = members.shape
    slots = groups // n * cap
    bound = 2 * tokens // n
    rows = n * bound
    vmem = pltpu.VMEM
    items = rounds * (groups // n)
    out = jax.ShapeDtypeStruct((tokens, feat), BF16)
    d_qk, d_values = pl.pallas_call(
        functools.partial(kernel, n, bound),
        out_shape=(out, out),
        in_specs=[pl.BlockSpec(memory_space=pltpu.HBM)] * 5,
        out_specs=(pl.BlockSpec(memory_space=vmem),) * 2,
        scratch_shapes=[
            vmem((cap // 128, rounds, groups, 128), jnp.int32),
            vmem((rounds, groups), jnp.int32),
            vmem((tokens, feat), BF16),
            vmem((tokens, feat), BF16),
            vmem((tokens, feat), BF16),
            vmem((rounds, n, bound, 2 * feat), BF16),
            vmem((rounds, n, bound, 2 * feat), BF16),
            vmem((rounds, n, bound, feat), BF16),
            vmem((rounds, n, bound, feat), BF16),
            vmem((n, 1, 128), F32),
            vmem((n, 1, 128), F32),
            vmem((n, 1, 128), F32),
            vmem((n, 1, 128), F32),
            vmem((rounds, cap, 2 * feat), BF16),
            vmem((rounds, cap, 2 * feat), BF16),
            vmem((rounds, n, bound, 2 * feat), BF16),
            vmem((rounds, n, bound, 2 * feat), BF16),
            vmem((rounds, rows, tokens), BF16),
            vmem((rounds, rows, slots), BF16),
            vmem((slots, slots), BF16),
            vmem((rounds, n, tokens), BF16),
            vmem((rounds, n, slots), BF16),
            vmem((128, rounds * tokens), BF16),
            vmem((128, rounds * slots), BF16),
            vmem((rounds, cap + slots, 2 * feat), BF16),
            vmem((rounds, slots, feat), BF16),
            vmem((rounds, cap + slots, feat), BF16),
            vmem((items, 2 * cap, cap), F32),
            vmem((items, 2 * cap, cap), F32),
            vmem((rounds, cap + slots, feat), F32),
            vmem((rounds, cap + slots, feat), F32),
            vmem((rounds, slots, feat), F32),
            pltpu.SemaphoreType.DMA((8,)),
            pltpu.SemaphoreType.DMA((8,)),
            pltpu.SemaphoreType.DMA((4,)),
            pltpu.SemaphoreType.DMA((4,)),
            pltpu.SemaphoreType.DMA((4 + cap // 128,)),
            pltpu.SemaphoreType.REGULAR,
        ],
        compiler_params=pltpu.CompilerParams(
            collective_id=0, has_side_effects=True, vmem_limit_bytes=66000000
        ),
        name="lsh_backward",
    )(members[0], counts[0], qk[0], values[0], grad_out[0])
    return d_qk[None], d_values[None]


def solution(mesh):
    rows = P("head", "seq", None)
    return jax.shard_map(
        on_device,
        mesh=mesh,
        in_specs=(rows, rows, rows, P("head", None, None, None), P("head", None, None)),
        out_specs=(rows, rows),
        check_vma=False,
    )
```

profile of v0, /device:TPU:1, one launch (start us, length us, event | category | flops | bytes accessed | tf_op | source)
XLA Modules:
  0.0 155.1 jit_solution(16360685933100582069)
XLA Ops:
  0.6 152.2 %lsh_backward.1 = (bf16[512,128]{1,0:T(8,128)(2,1)}, bf16[512,128]{1,0:T(8,128)(2,1)}) custom-call(s32[2,192,256]{2,1,0:T(8,128)} %bitcast.7, s32[2,192]{1,0:T(2,128)} %bitcast.13, bf16[512,128]{1,0:T(8,128)(2,1)} %bitcast.10, bf16[512,128]{1,0:T(8,128)(2,1)} %bitcast.11, bf16[512,128]{1,0:T(8,128)(2,1)} %bitcast.12), custom_call_target="tpu_custom_call" | custom-call | tf_op jit(solution)/shard_map/lsh_backward/pallas_call | solution.py:390
  152.8 0.0 copy-start
  152.9 1.6 %copy.9 = bf16[1,512,128]{2,1,0:T(8,128)(2,1)} copy(bf16[1,512,128]{2,1,0:T(8,128)(2,1)} %bitcast.9) | data formatting | bytes 262144
  154.5 0.0 copy-done
  154.5 0.7 copy.10
Async XLA Ops:
  152.8 1.6 %copy-start = (bf16[512,128]{1,0:T(8,128)(2,1)S(1)}, bf16[512,128]{1,0:T(8,128)(2,1)}, u32[]{:S(2)}) copy-start(bf16[512,128]{1,0:T(8,128)(2,1)} %get-tuple-element.5) | copy-start | bytes 393220
where the time goes:
time: 155 us
  Pallas kernels  152 us (98%)
  local copies, waits for them, and re-layouts  2.26 us (1%)
    pallas_call x1, Pallas kernels, on_device(): pl.pallas_call(functools.partial(kernel, n, bound), out_shape=(out, out),...  152 us

commit v1 on v0

--- a/solution.py
+++ b/solution.py
@@ -347,7 +347,6 @@
 
     for r in range(rounds):
         backward(r, 0)
-    for r in range(rounds):
         near(se.at[r], re.at[r], rounds + r, previous).start()
     for r in range(rounds):
         for c in range(1, per):
@@ -433,10 +432,15 @@
             pltpu.SemaphoreType.REGULAR,
         ],
         compiler_params=pltpu.CompilerParams(
-            collective_id=0, has_side_effects=True, vmem_limit_bytes=66000000
+            collective_id=0, has_side_effects=True, vmem_limit_bytes=36 * 1024 * 1024
         ),
         name="lsh_backward",
-    )(members[0], counts[0], qk[0], values[0], grad_out[0])
+    )(
+        *(
+            pltpu.with_memory_space_constraint(x[0], pltpu.HBM)
+            for x in (members, counts, qk, values, grad_out)
+        )
+    )
     return d_qk[None], d_values[None]
 
 

time: 155 us -> 153 us (0.987)
  no operation moved by 1% of the time
where the time goes in v1:
time: 153 us
  Pallas kernels  151 us (99%)
    pallas_call x1, Pallas kernels, on_device(): pl.pallas_call(functools.partial(kernel, n, bound), out_shape=(out, out),...  151 us

profile of v1, /device:TPU:1, one launch (start us, length us, event | category | flops | bytes accessed | tf_op | source)
XLA Modules:
  0.0 153.2 jit_solution(10264347613577700476)
XLA Ops:
  0.6 151.2 %lsh_backward.1 = (bf16[512,128]{1,0:T(8,128)(2,1)S(1)}, bf16[512,128]{1,0:T(8,128)(2,1)S(1)}) custom-call(s32[2,192,256]{2,1,0:T(8,128)} %bitcast.9, s32[2,192]{1,0:T(2,128)} %bitcast.13, bf16[512,128]{1,0:T(8,128)(2,1)} %bitcast.10, bf16[512,128]{1,0:T(8,128)(2,1)} %bitcast.11, bf16[512,128]{1,0:T(8,128)(2,1)} %bitcast.12), custom_call_target="tpu_custom_call" | custom-call | tf_op jit(solution)/shard_map/lsh_backward/pallas_call | solution.py:389
  151.9 0.7 copy.9
  152.5 0.7 copy.10
